TPU v7x, 128 devices: a whole 4x4x4 slice. The times are simulated.
128 devices in a mesh: sec: 2 (over y_hi), dev: 32 (over z, x, core), tp: 2 (over y_lo).
Axes of the slice: x: 4, y: 4 (y_hi: 2, y_lo: 2; y = y_hi * 2 + y_lo), z: 4, core: 2. Of those that a mesh axis runs over, the one named last changes fastest.
Arguments:
- queries: bfloat16 [512, 8192], P(('sec', 'dev'), 'tp'), may hold values from -6 to 6
- new_keys: bfloat16 [512, 1024], P(('sec', 'dev'), 'tp'), may hold values from -6 to 6
- token_values: bfloat16 [512, 1024], P(('sec', 'dev'), 'tp'), may hold values from -6 to 6
- key_cache: bfloat16 [512, 256, 1024], P(('sec', 'dev'), None, 'tp'), may hold values from -6 to 6
- stored_values: bfloat16 [512, 256, 1024], P(('sec', 'dev'), None, 'tp'), may hold values from -6 to 6
- cache_lengths: int32 [512], P(('sec', 'dev')), may hold values from 1 to 256, 65536 in all
- residual: bfloat16 [512, 8192], P(('sec', 'dev', 'tp')), may hold values from -6 to 6
- norm_gain: float32 [8192], replicated, may hold values from 0.25 to 1.75
- active: int32 [512, 16], P(('sec', 'dev', 'tp')), may hold values from 0 to 127, all different within a row; in each aligned block of 4 rows (0 to 3, 4 to 7, ...) at most 3 rows name the same one
- gate_weight: bfloat16 [8192, 16384], P(None, ('sec', 'dev', 'tp')), may hold values from -0.0625 to 0.0625
- up_weight: bfloat16 [8192, 16384], P(None, ('sec', 'dev', 'tp')), may hold values from -0.0625 to 0.0625
- down_weight: bfloat16 [16384, 8192], P(('sec', 'dev', 'tp')), may hold values from -0.125 to 0.125
Outputs:
- layer_out: bfloat16 [512, 8192], P(('sec', 'dev', 'tp'))
Inputs may be any that keep to these rules, and one draw needn't show every extreme that they name: `cache_lengths`: the largest length is 256 in every draw. `active`: the bundles of one row are distinct. Among the 4 rows of one device (aligned blocks of rows), no bundle is named by more than 3 rows, and some bundle reaches 3.
All inputs are finite; a program needn't handle non-finite values. No bound on the sum of `cache_lengths` on one device may be relied on, other than what follows from the above.
Results may differ from a plain program's by a relative error of at most 0.007.
Values may be sent and summed in bfloat16 or wider, within the bound.
A program may use at most 128 MiB of HBM per device.

v0:
```python
import jax
import jax.numpy as jnp
from jax import lax
from jax.sharding import PartitionSpec as P

HEAD_SIZE = 128
CACHE_POSITIONS = 256
epsilon = 1e-05


def attend(queries, new_keys, token_values, key_cache, stored_values, cache_lengths):
    request_count, query_width = queries.shape
    kv_width = new_keys.shape[1]
    kv_heads = kv_width // HEAD_SIZE
    group_width = query_width // kv_width
    scaling = HEAD_SIZE ** (-0.5)
    grouped = queries.reshape(request_count, kv_heads, group_width, HEAD_SIZE)
    cached_keys = key_cache.reshape(request_count, CACHE_POSITIONS, kv_heads, HEAD_SIZE)
    cached_values = stored_values.reshape(request_count, CACHE_POSITIONS, kv_heads, HEAD_SIZE)
    scores = (
        jnp.einsum("rkgd,rckd->rkgc", grouped, cached_keys, preferred_element_type=jnp.float32)
        * scaling
    )
    visible = jnp.arange(CACHE_POSITIONS, dtype=jnp.int32)[None, :] < cache_lengths[:, None]
    scores = jnp.where(visible[:, None, None, :], scores, -jnp.inf)
    fresh_keys = new_keys.reshape(request_count, kv_heads, HEAD_SIZE)
    fresh_score = (
        jnp.einsum("rkgd,rkd->rkg", grouped, fresh_keys, preferred_element_type=jnp.float32)
        * scaling
    )
    highest = jnp.maximum(jnp.max(scores, axis=-1), fresh_score)
    weights_cache = jnp.exp(scores - highest[..., None])
    weight_fresh = jnp.exp(fresh_score - highest)
    denominator = jnp.sum(weights_cache, axis=-1) + weight_fresh
    probs_cache = (weights_cache / denominator[..., None]).astype(jnp.bfloat16)
    prob_fresh = (weight_fresh / denominator).astype(jnp.bfloat16)
    blended = jnp.einsum(
        "rkgc,rckd->rkgd", probs_cache, cached_values, preferred_element_type=jnp.float32
    )
    fresh_values = token_values.reshape(request_count, kv_heads, 1, HEAD_SIZE).astype(jnp.float32)
    blended = blended + prob_fresh[..., None].astype(jnp.float32) * fresh_values
    return blended.reshape(request_count, query_width).astype(jnp.bfloat16)


def feed_forward(row_block, gate_weight, up_weight, selected):
    gate_value = jnp.dot(row_block, gate_weight, preferred_element_type=jnp.float32)
    up_value = jnp.dot(row_block, up_weight, preferred_element_type=jnp.float32)
    return (jax.nn.relu(gate_value) * up_value * selected).astype(jnp.bfloat16)


def shards(
    queries,
    new_keys,
    token_values,
    key_cache,
    stored_values,
    cache_lengths,
    residual,
    norm_gain,
    active,
    gate_weight,
    up_weight,
    down_weight,
):
    context = attend(queries, new_keys, token_values, key_cache, stored_values, cache_lengths)
    context = lax.all_to_all(context, "tp", split_axis=0, concat_axis=1, tiled=True)
    stream = residual.astype(jnp.float32) + context.astype(jnp.float32)
    mean_square = jnp.mean(stream * stream, axis=1, keepdims=True)
    normed = (stream * lax.rsqrt(mean_square + epsilon) * norm_gain[None, :]).astype(jnp.bfloat16)
    axes = ("sec", "dev", "tp")
    bundle = lax.axis_index(axes)
    named = jnp.any(active[:, :, None] == jnp.arange(128, dtype=jnp.int32)[None, None, :], axis=1)
    packed = jnp.concatenate([normed, named.astype(jnp.bfloat16)], axis=1)
    gathered = lax.all_gather(packed, axes, axis=0, tiled=True)
    rows = gathered[:, :8192]
    wanted = jnp.sum(
        jnp.where(jnp.arange(128)[None, :] == bundle, gathered[:, 8192:].astype(jnp.float32), 0.0),
        axis=1,
        keepdims=True,
    )
    hidden = feed_forward(rows, gate_weight, up_weight, wanted)
    terms = jnp.dot(hidden, down_weight, preferred_element_type=jnp.float32).astype(jnp.bfloat16)
    terms = terms.reshape(128, 32, 1024)
    update = lax.psum_scatter(terms, axes, scatter_dimension=0, tiled=False).reshape(4, 8192)
    return (stream + update.astype(jnp.float32)).astype(jnp.bfloat16)


def solution(mesh):
    return jax.shard_map(
        shards,
        mesh=mesh,
        in_specs=(
            P(("sec", "dev"), "tp"),
            P(("sec", "dev"), "tp"),
            P(("sec", "dev"), "tp"),
            P(("sec", "dev"), None, "tp"),
            P(("sec", "dev"), None, "tp"),
            P(("sec", "dev")),
            P(("sec", "dev", "tp"), None),
            P(),
            P(("sec", "dev", "tp"), None),
            P(None, ("sec", "dev", "tp")),
            P(None, ("sec", "dev", "tp")),
            P(("sec", "dev", "tp"), None),
        ),
        out_specs=P(("sec", "dev", "tp"), None),
        check_vma=False,
    )
```

profile of v0, /device:TPU:0, one launch (start us, length us, event | category | flops | bytes accessed | tf_op | source)
XLA Modules:
  0.0 1051.2 jit_solution(6356441522327722411)
XLA Ops:
  6.5 0.0 copy-start
  6.5 0.0 copy-start.4
  6.5 0.9 iota_compare_fusion.1
  7.4 0.8 bitcast_convert_fusion
  8.2 1.0 fusion.41
  9.2 2.4 fusion.49
  11.6 0.0 copy-start.3
  11.6 0.2 fusion.36
  11.8 0.0 copy-start.1
  11.9 0.0 copy-start.2
  11.9 0.0 copy-done.4
  11.9 0.5 fusion.33
  12.4 0.7 convert_element_type.71
  13.0 3.3 all-to-all-start
  16.3 0.0 all-gather.3.cloned.1.call-start
  16.4 0.0 copy-done.3
  16.4 0.1 fusion.44
  16.5 3.9 all-to-all-done
  20.5 0.0 copy-done.1
  20.5 0.2 multiply_reduce_fusion
  20.7 0.0 copy-done.2
  20.7 0.1 multiply_convert_fusion
  20.8 0.6 maximum_bitcast_fusion
  21.4 0.0 all-gather.3.cloned.1.call-update
  21.4 0.0 reduce-scatter.2.cloned.1.call-start
  21.5 311.8 %all-gather.3.cloned.1.call-done = bf16[128,4,8320]{2,1,0:T(4,128)(2,1)} async-done(((bf16[1,4,8320]{2,1,0:T(4,128)(2,1)}), bf16[128,4,8320]{2,1,0:T(4,128)(2,1)}) %all-gather.3.cloned.1.call-update) | async-done | bytes 8519696 | tf_op jit(solution)/shard_map/all_gather | solution.py:74
  333.3 12.6 %reshape.81 = bf16[512,8320]{1,0:T(8,128)(2,1)} reshape(bf16[128,4,8320]{2,1,0:T(4,128)(2,1)} %all-gather.3.cloned.1.call-done) | data formatting | bytes 17039360
  345.9 1.0 select_reduce_fusion
  346.9 6.3 fusion
  353.2 0.0 copy-done
  353.2 17.2 %convolution_convert_fusion = bf16[512,8192]{1,0:T(8,128)(2,1)} fusion(bf16[128,8192]{1,0:T(8,128)(2,1)S(1)} %copy-done, f32[512,128]{1,0:T(8,128)S(1)} %fusion, bf16[8192,128]{1,0:T(8,128)(2,1)} %param.21, bf16[512,8320]{1,0:T(8,128)(2,1)} %reshape.81, f32[512]{0:T(512)S(1)} %select_reduce_fusion), kind=kOutput, calls=%fused_computation | convolution fusion | flops 2151940096 | bytes 21235712 | tf_op jit(solution)/shard_map/dot_general | solution.py:82
  370.4 13.5 %reshape.76 = bf16[128,32,1024]{2,1,0:T(8,128)(2,1)} reshape(bf16[512,8192]{1,0:T(8,128)(2,1)} %convolution_convert_fusion) | data formatting | bytes 16777216 | tf_op jit(solution)/shard_map/reshape | solution.py:83
  383.9 0.0 reduce-scatter.2.cloned.1.call-update
  383.9 658.9 %reduce-scatter.2.cloned.1.call-done = bf16[1,32,1024]{2,1,0:T(8,128)(2,1)} async-done(((bf16[128,32,1024]{2,1,0:T(8,128)(2,1)}), bf16[1,32,1024]{2,1,0:T(8,128)(2,1)}) %reduce-scatter.2.cloned.1.call-update) | async-done | bytes 65552 | tf_op jit(solution)/shard_map/reduce_scatter | solution.py:84
  1042.8 0.9 reshape.79
  1043.7 0.7 add_convert_fusion
  (7 shorter events, 0.1 us)
Async XLA Ops:
  6.5 346.7 %copy-start = (bf16[128,8192]{1,0:T(8,128)(2,1)S(1)}, bf16[128,8192]{1,0:T(8,128)(2,1)}, u32[]{:S(2)}) copy-start(bf16[128,8192]{1,0:T(8,128)(2,1)} %param.23) | copy-start | bytes 6291460
  6.5 5.4 copy-start.4
  11.6 4.8 copy-start.3
  11.8 8.6 copy-start.1
  11.9 8.8 copy-start.2
  13.0 7.4 all-to-all-start
  16.3 317.0 %all-gather.3.cloned.1.call-start = ((), (), s32[]{:S(2)}) async-start(), calls=%async_computation.3 | async-start | bytes 8586240 | tf_op jit(solution)/shard_map/all_gather | solution.py:74
  21.4 1021.3 %reduce-scatter.2.cloned.1.call-start = ((), (), s32[]{:S(2)}) async-start(), calls=%async_computation.2 | async-start | bytes 8454144 | tf_op jit(solution)/shard_map/reduce_scatter | solution.py:84
Sparse Core Ops, SparseCore 0:
  21.6 311.6 all-gather.2
  384.0 658.6 reduce-scatter.1
where the time goes:
time: 1050 us
  waiting for transfers between devices  975 us (93%)
  local copies, waits for them, and re-layouts  27.7 us (3%)
  matrix products  27.3 us (3%)
  between operations  13.5 us (1%)
    reduce_scatter x1, waiting for transfers between devices, shards(): lax.psum_scatter(terms, axes, scatter_dimension=0, tiled=False)  659 us
    all_gather x1, waiting for transfers between devices, shards(): gathered = lax.all_gather(packed, axes, axis=0, tiled=True)  312 us
  transfers between devices with their start and end apart: 3, of which 3 were waited for; matrix products, arithmetic and copies ran while one was open for 0% of the time, Pallas kernels for 0%

commit v1 on v0

--- a/solution.py
+++ b/solution.py
@@ -71,7 +71,8 @@
     bundle = lax.axis_index(axes)
     named = jnp.any(active[:, :, None] == jnp.arange(128, dtype=jnp.int32)[None, None, :], axis=1)
     packed = jnp.concatenate([normed, named.astype(jnp.bfloat16)], axis=1)
-    gathered = lax.all_gather(packed, axes, axis=0, tiled=True)
+    repeated = jnp.stack([packed] * lax.axis_size(axes))
+    gathered = jnp.concatenate(lax.all_to_all(repeated, axes, 0, 0), axis=0)
     rows = gathered[:, :8192]
     wanted = jnp.sum(
         jnp.where(jnp.arange(128)[None, :] == bundle, gathered[:, 8192:].astype(jnp.float32), 0.0),

time: 1050 us -> 871 us (0.83)
  waiting for transfers between devices: 975 us -> 777 us
  starting transfers between devices: 3.38 us -> 15 us
    all_gather x1 -> x0, waiting for transfers between devices: 312 us -> none  [shards(): gathered = lax.all_gather(packed, axes, axis=0, tiled=True)]
    all_to_all x0 -> x1, waiting for transfers between devices: none -> 103 us  [shards(): gathered = jnp.concatenate(lax.all_to_all(repeated, axes, 0, 0), axis=0)]
    reshape x0 -> x1, local copies, waits for them, and re-layouts: none -> 12.6 us  [shards(): gathered = jnp.concatenate(lax.all_to_all(repeated, axes, 0, 0), axis=0)]
    unnamed x11 -> x10, local copies, waits for them, and re-layouts: 12.6 us -> 0.02 us
    all_to_all x0 -> x1, starting transfers between devices: none -> 11.6 us  [shards(): gathered = jnp.concatenate(lax.all_to_all(repeated, axes, 0, 0), axis=0)]
    reduce_scatter x1, waiting for transfers between devices: 659 us -> 670 us  [shards(): lax.psum_scatter(terms, axes, scatter_dimension=0, tiled=False)]
where the time goes in v1:
time: 871 us; the launch traced here: 870 us
  waiting for transfers between devices  777 us (89%)
  local copies, waits for them, and re-layouts  33.2 us (4%)
  matrix products  27.3 us (3%)
  starting transfers between devices  15 us (2%)
  between operations  13.5 us (2%)
    reduce_scatter x1, waiting for transfers between devices, shards(): lax.psum_scatter(terms, axes, scatter_dimension=0, tiled=False)  670 us
    all_to_all x1, waiting for transfers between devices, shards(): gathered = jnp.concatenate(lax.all_to_all(repeated, axes, 0, 0), axis=0)  103 us
  transfers between devices with their start and end apart: 3, of which 3 were waited for; matrix products, arithmetic and copies ran while one was open for 0% of the time, Pallas kernels for 0%

profile of v1, /device:TPU:0, one launch (start us, length us, event | category | flops | bytes accessed | tf_op | source)
XLA Modules:
  0.0 869.6 jit_solution(441742927683370989)
XLA Ops:
  6.5 0.0 copy-start
  6.5 0.0 copy-start.4
  6.5 0.9 iota_compare_fusion.1
  7.4 0.8 bitcast_convert_fusion
  8.2 1.0 fusion.41
  9.2 2.4 fusion.49
  11.6 0.0 copy-start.3
  11.6 0.2 fusion.36
  11.8 0.0 copy-start.1
  11.9 0.0 copy-start.2
  11.9 0.0 copy-done.4
  11.9 0.5 fusion.33
  12.4 0.7 convert_element_type.71
  13.0 3.3 all-to-all-start
  16.3 0.0 copy-done.3
  16.3 0.1 fusion.44
  16.5 4.0 all-to-all-done
  20.5 0.0 copy-done.1
  20.5 0.2 multiply_reduce_fusion
  20.7 0.0 copy-done.2
  20.7 0.1 multiply_convert_fusion
  20.8 5.5 stack.2
  26.3 11.6 %all-to-all-start.1 = ((bf16[128,4,8320]{2,1,0:T(4,128)(2,1)}), bf16[128,4,8320]{2,1,0:T(4,128)(2,1)}, u32[]{:S(2)}, u32[]{:S(2)}) async-start(bf16[128,4,8320]{2,1,0:T(4,128)(2,1)} %stack.2), calls=%async_computation.1 | async-start | bytes 17039360 | tf_op jit(solution)/shard_map/all_to_all | solution.py:75
  37.9 0.0 reduce-scatter.2.cloned.1.call-start
  38.0 102.9 %all-to-all-done.1 = bf16[128,4,8320]{2,1,0:T(4,128)(2,1)} async-done(((bf16[128,4,8320]{2,1,0:T(4,128)(2,1)}), bf16[128,4,8320]{2,1,0:T(4,128)(2,1)}, u32[]{:S(2)}, u32[]{:S(2)}) %all-to-all-start.1) | async-done | bytes 8519712 | tf_op jit(solution)/shard_map/all_to_all | solution.py:75
  140.9 12.6 %reshape.81 = bf16[512,8320]{1,0:T(8,128)(2,1)} reshape(bf16[128,4,8320]{2,1,0:T(4,128)(2,1)} %all-to-all-done.1) | data formatting | bytes 17039360 | tf_op jit(solution)/shard_map/reshape | solution.py:75
  153.5 1.0 select_reduce_fusion
  154.5 6.3 fusion
  160.8 0.0 copy-done
  160.8 17.2 %convolution_convert_fusion = bf16[512,8192]{1,0:T(8,128)(2,1)} fusion(bf16[128,8192]{1,0:T(8,128)(2,1)S(1)} %copy-done, f32[512,128]{1,0:T(8,128)S(1)} %fusion, bf16[8192,128]{1,0:T(8,128)(2,1)} %param.21, bf16[512,8320]{1,0:T(8,128)(2,1)} %reshape.81, f32[512]{0:T(512)S(1)} %select_reduce_fusion), kind=kOutput, calls=%fused_computation | convolution fusion | flops 2151940096 | bytes 21235712 | tf_op jit(solution)/shard_map/dot_general | solution.py:83
  178.0 13.5 %reshape.82 = bf16[128,32,1024]{2,1,0:T(8,128)(2,1)} reshape(bf16[512,8192]{1,0:T(8,128)(2,1)} %convolution_convert_fusion) | data formatting | bytes 16777216 | tf_op jit(solution)/shard_map/reshape | solution.py:84
  191.5 0.0 reduce-scatter.2.cloned.1.call-update
  191.5 669.6 %reduce-scatter.2.cloned.1.call-done = bf16[1,32,1024]{2,1,0:T(8,128)(2,1)} async-done(((bf16[128,32,1024]{2,1,0:T(8,128)(2,1)}), bf16[1,32,1024]{2,1,0:T(8,128)(2,1)}) %reduce-scatter.2.cloned.1.call-update) | async-done | bytes 65552 | tf_op jit(solution)/shard_map/reduce_scatter | solution.py:85
  861.1 0.9 reshape.85
  862.1 0.7 add_convert_fusion
  (8 shorter events, 0.1 us)
Async XLA Ops:
  6.5 154.3 %copy-start = (bf16[128,8192]{1,0:T(8,128)(2,1)S(1)}, bf16[128,8192]{1,0:T(8,128)(2,1)}, u32[]{:S(2)}) copy-start(bf16[128,8192]{1,0:T(8,128)(2,1)} %param.23) | copy-start | bytes 6291460
  6.5 5.4 copy-start.4
  11.6 4.7 copy-start.3
  11.8 8.6 copy-start.1
  11.9 8.8 %copy-start.2 = (f32[8192]{0:T(1024)S(1)}, f32[8192]{0:T(1024)}, u32[]{:S(2)}) copy-start(f32[8192]{0:T(1024)} %param.19) | copy-start | bytes 98308
  13.0 7.4 all-to-all-start
  26.3 114.6 %all-to-all-start.1 = ((bf16[128,4,8320]{2,1,0:T(4,128)(2,1)}), bf16[128,4,8320]{2,1,0:T(4,128)(2,1)}, u32[]{:S(2)}, u32[]{:S(2)}) async-start(bf16[128,4,8320]{2,1,0:T(4,128)(2,1)} %stack.2), calls=%async_computation.1 | async-start | bytes 17039360 | tf_op jit(solution)/shard_map/all_to_all | solution.py:75
  37.9 823.2 %reduce-scatter.2.cloned.1.call-start = ((), (), s32[]{:S(2)}) async-start(), calls=%async_computation.3 | async-start | bytes 8454144 | tf_op jit(solution)/shard_map/reduce_scatter | solution.py:85
Sparse Core Ops, SparseCore 0:
  191.6 669.4 reduce-scatter.1
